TPU v7x, 256 devices: a whole 4x4x8 slice. The times are simulated.
256 devices in a mesh: dp: 16 (over y, x), mem: 16 (over z, core).
Axes of the slice: x: 4, y: 4, z: 8, core: 2. Of those that a mesh axis runs over, the one named last changes fastest.
Arguments:
- grad_out: bfloat16 [2048, 4096], P('dp', 'mem'), may hold values from -16 to 16
- values: bfloat16 [4096, 4096], P('dp', 'mem'), may hold values from -0.0234375 to 0.0234375
- slot_rows: int32 [2048, 32], P('dp'), may hold values from 0 to 4095, all different within a row
- weights: float32 [2048, 32], P('dp'), may hold values from 0 to 1, as said below
- sub_picks: int32 [2, 2048, 32], P(None, 'dp'), may hold values from 0 to 1023
- queries: bfloat16 [2048, 1024], P('dp'), may hold values from -6 to 6
- sub_keys: bfloat16 [2, 1024, 512], replicated, may hold values from -0.25 to 0.25
- layer_input: bfloat16 [2048, 4096], P('dp', 'mem'), may hold values from -6 to 6
Outputs:
- value_grad: float32 [4096, 4096], P('dp', 'mem')
- key_grad: float32 [2, 1024, 512], P(None, 'dp')
- proj_grad: float32 [1024, 4096], P('dp', 'mem')
Inputs may be any that keep to these rules, and one draw needn't show every extreme that they name: `slot_rows`: the 32 value rows of one token are distinct, and every value row is read by some token. Each token's 32 weights are positive and sum to one.
All inputs are finite; a program needn't handle non-finite values.
Results may differ from a plain program's by a relative error of at most 0.004.
Values may be sent and summed in bfloat16 or wider, within the bound.
No kernel may reach another device: no remote copies, remote signals or barrier semaphores. Data moves between devices by JAX's collectives and lax.ppermute only.
A program may use at most 64 MiB of HBM per device.

v0:
```python
import jax
import jax.numpy as jnp
from jax import lax
from jax.sharding import PartitionSpec as P

highest = lax.Precision.HIGHEST


def split_hot(offsets, blocks, block_width, table_type):
    inside_mask = (offsets >= 0) & (offsets < blocks * block_width)
    clipped = jnp.where(inside_mask, offsets, 0)
    block_ids = clipped // block_width
    within_ids = clipped - block_ids * block_width
    block_hot = (
        (block_ids[:, :, None] == jnp.arange(blocks, dtype=jnp.int32)) & inside_mask[:, :, None]
    ).astype(table_type)
    within_hot = (within_ids[:, :, None] == jnp.arange(block_width, dtype=jnp.int32)).astype(
        table_type
    )
    return (block_hot, within_hot)


def value_block(grad_rows, row_ids, row_weights, values, owner_start):
    val_rows = values.shape[0]
    blocks = val_rows // 128
    row_count = grad_rows.shape[0]
    block_hot, within_hot = split_hot(row_ids - owner_start, blocks, 128, jnp.bfloat16)
    weighted = block_hot * row_weights[:, :, None]
    bag_wide = jnp.einsum("tkb,tkc->tbc", weighted, within_hot, preferred_element_type=jnp.float32)
    bag_rows = bag_wide.reshape(row_count, val_rows).astype(jnp.bfloat16)
    value_term = lax.dot_general(
        bag_rows, grad_rows, (((0,), (0,)), ((), ())), preferred_element_type=jnp.float32
    )
    scores = lax.dot_general(
        grad_rows, values, (((1,), (1,)), ((), ())), preferred_element_type=jnp.float32
    )
    scores = scores.reshape(row_count, blocks, 128)
    picked = jnp.einsum(
        "tbc,tkb->tkc",
        scores,
        block_hot.astype(jnp.float32),
        precision=highest,
        preferred_element_type=jnp.float32,
    )
    slot_term = jnp.sum(picked * within_hot.astype(jnp.float32), axis=2)
    return (value_term, slot_term)


def body(grad_out, values, slot_rows, weights, sub_picks, queries, sub_keys, layer_input):
    val_rows = values.shape[0]
    slot_count = slot_rows.shape[1]
    groups = lax.axis_size("dp")
    owner_start = lax.axis_index("dp") * val_rows
    vweights = weights.astype(jnp.bfloat16)
    start_acc = jnp.zeros((val_rows, values.shape[1]), jnp.float32)
    value_acc = start_acc
    grad_rows = lax.all_gather(grad_out, "dp", axis=0, tiled=True)
    row_ids = lax.all_gather(slot_rows, "dp", axis=0, tiled=True)
    row_weights = lax.all_gather(vweights, "dp", axis=0, tiled=True)
    row_count = grad_rows.shape[0]
    block_rows = 512
    steps_count = row_count // block_rows

    def one_block(acc_now, blocked):
        value_term, slot_term = value_block(blocked[0], blocked[1], blocked[2], values, owner_start)
        return (acc_now + value_term, slot_term)

    stacked = (
        grad_rows.reshape(steps_count, block_rows, grad_rows.shape[1]),
        row_ids.reshape(steps_count, block_rows, slot_count),
        row_weights.reshape(steps_count, block_rows, slot_count),
    )
    value_acc, slot_terms = lax.scan(one_block, value_acc, stacked)
    slot_all = slot_terms.reshape(row_count, slot_count)
    value_grad, slot_all = (value_acc, slot_all)
    slot_grad = lax.psum(lax.psum_scatter(slot_all, "dp", scatter_dimension=0, tiled=True), "mem")
    centered = slot_grad - jnp.sum(weights * slot_grad, axis=1, keepdims=True)
    score_grad = weights * centered
    own_count = score_grad.shape[0]
    sub_count = sub_keys.shape[1]
    key_width = sub_keys.shape[2]
    sub_width = 128
    halves = []
    for half_index in range(2):
        block_hot, within_hot = split_hot(
            sub_picks[half_index], sub_count // sub_width, sub_width, jnp.float32
        )
        weighted = block_hot * score_grad[:, :, None]
        summed = jnp.einsum(
            "tkb,tkc->tbc",
            weighted,
            within_hot,
            precision=highest,
            preferred_element_type=jnp.float32,
        )
        halves.append(summed.reshape(own_count, sub_count))
    sub_grad = jnp.stack(halves, axis=1).astype(jnp.bfloat16)
    query_pairs = queries.reshape(own_count, 2, key_width)
    mem_count = lax.axis_size("mem")
    piece_rows = sub_count // (groups * mem_count)
    sub_view = sub_grad.reshape(own_count, 2, groups, mem_count, piece_rows)
    own_piece = lax.dynamic_slice_in_dim(sub_view, lax.axis_index("mem"), 1, 3)
    key_source = own_piece.reshape(own_count, 2, groups * piece_rows)
    key_part = jnp.einsum(
        "thc,the->hce", key_source, query_pairs, preferred_element_type=jnp.float32
    )
    dquery = jnp.einsum("thc,hce->the", sub_grad, sub_keys, preferred_element_type=jnp.float32)
    dquery = dquery.reshape(own_count, 2 * key_width).astype(jnp.bfloat16)
    key_grad = lax.psum_scatter(key_part, "dp", scatter_dimension=1, tiled=True)
    proj_grad = lax.psum_scatter(
        lax.dot_general(
            dquery, layer_input, (((0,), (0,)), ((), ())), preferred_element_type=jnp.float32
        ),
        "dp",
        scatter_dimension=0,
        tiled=True,
    )
    key_grad = lax.all_gather(key_grad, "mem", axis=1, tiled=True)
    return (value_grad, key_grad, proj_grad)


def solution(mesh):
    return jax.shard_map(
        body,
        mesh=mesh,
        in_specs=(
            P("dp", "mem"),
            P("dp", "mem"),
            P("dp", None),
            P("dp", None),
            P(None, "dp", None),
            P("dp", None),
            P(),
            P("dp", "mem"),
        ),
        out_specs=(P("dp", "mem"), P(None, "dp", None), P("dp", "mem")),
        check_vma=False,
    )
```

profile of v0, /device:TPU:2, one launch (start us, length us, event | category | flops | bytes accessed | tf_op | source)
XLA Modules:
  0.0 467.8 jit_solution(13477727605715217793)
XLA Ops:
  7.2 0.7 all-gather.2.cloned.1.call-update
  8.0 25.9 %all_gather.12 = s32[2048,32]{0,1:T(8,128)} all-gather(s32[128,32]{0,1:T(8,128)} %param.12), channel_id=1, replica_groups=mesh['dp'=16,'mem'=16] {'dp'}, dimensions={0}, use_global_device_ids=true | all-gather | bytes 278528 | tf_op jit(solution)/shard_map/all_gather | solution.py:58
  33.8 1.3 copy.38
  35.1 0.7 convert_element_type.41
  35.9 22.0 %all_gather.13 = bf16[2048,32]{0,1:T(8,128)(2,1)S(1)} all-gather(bf16[128,32]{0,1:T(8,128)(2,1)S(1)} %convert_element_type.41), channel_id=1, replica_groups=mesh['dp'=16,'mem'=16] {'dp'}, dimensions={0}, use_global_device_ids=true | all-gather | bytes 139264 | tf_op jit(solution)/shard_map/all_gather | solution.py:59
  57.8 1.0 copy.39
  58.9 1.7 all-gather.2.cloned.1.call-done
  60.5 90.1 %while.15 = (s32[]{:T(128)}, f32[256,256]{1,0:T(8,128)S(1)}, f32[4,512,32]{2,1,0:T(8,128)}, s32[4,512,32]{2,1,0:T(8,128)S(1)}, s32[]{:T(128)}, /*index=5*/bf16[4...) while((s32[]{:T(128)}, f32[256,256]{1,0:T(8,128)S(1)}, ...), condition=%wide.region_2.3_spmd.clone, body=%wide.region_0.2_spmd.clone.sunk | while | flops 206569472 | bytes 4358351 | solution.py:73
  61.0 1.0 dynamic-slice_bitcast_fusion.2
  62.0 4.8 %fusion.85 = bf16[512,2,128]{2,1,0:T(2,128)(2,1)} fusion(s32[512,32]{1,0:T(8,128)S(1)} %multiply_subtract_fusion.4, pred[512,32]{1,0:T(8,128)(4,1)S(1)} %get-tuple-element.212, s32[512,32]{1,0:T(8,128)S(1)} %get-tuple-element.213, bf16[512,32]{1,0:T(8,128)(2,1)S(1)} %dynamic-slice_bitcast_fusion.2), kind=kOutput, calls=%fused_computation.5.clone.1 | convolution fusion | flops 10715136 | bytes 442368 | tf_op jit(solution)/shard_map/while/body/eval_jaxpr/tkb,tkc->tbc/dot_general | solution.py:29
  66.8 1.3 convolution_add_fusion.2
  68.1 1.2 fusion.86
  69.4 13.0 %multiply_reduce_fusion.3 = f32[512,32]{1,0:T(8,128)S(1)} fusion(s32[512,32]{1,0:T(8,128)} %copy-done.3, f32[512,2,128]{2,0,1:T(8,128)S(1)} %fusion.86, pred[512,32]{1,0:T(8,128)(4,1)S(1)} %get-tuple-element.212, s32[512,32]{1,0:T(8,128)} %copy-done.2), kind=kOutput, calls=%fused_computation.clone.1 | convolution fusion | flops 60866560 | bytes 737280 | tf_op jit(solution)/shard_map/while/body/eval_jaxpr/tbc,tkb->tkc/dot_general | solution.py:38
  82.3 0.7 bitcast_dynamic-update-slice_fusion.2
  83.5 1.0 dynamic-slice_bitcast_fusion.2
  84.5 4.8 %fusion.85 = bf16[512,2,128]{2,1,0:T(2,128)(2,1)} fusion(s32[512,32]{1,0:T(8,128)S(1)} %multiply_subtract_fusion.4, pred[512,32]{1,0:T(8,128)(4,1)S(1)} %get-tuple-element.212, s32[512,32]{1,0:T(8,128)S(1)} %get-tuple-element.213, bf16[512,32]{1,0:T(8,128)(2,1)S(1)} %dynamic-slice_bitcast_fusion.2), kind=kOutput, calls=%fused_computation.5.clone.1 | convolution fusion | flops 10715136 | bytes 442368 | tf_op jit(solution)/shard_map/while/body/eval_jaxpr/tkb,tkc->tbc/dot_general | solution.py:29
  89.3 1.3 convolution_add_fusion.2
  90.6 1.2 fusion.86
  91.9 13.0 %multiply_reduce_fusion.3 = f32[512,32]{1,0:T(8,128)S(1)} fusion(s32[512,32]{1,0:T(8,128)} %copy-done.3, f32[512,2,128]{2,0,1:T(8,128)S(1)} %fusion.86, pred[512,32]{1,0:T(8,128)(4,1)S(1)} %get-tuple-element.212, s32[512,32]{1,0:T(8,128)} %copy-done.2), kind=kOutput, calls=%fused_computation.clone.1 | convolution fusion | flops 60866560 | bytes 737280 | tf_op jit(solution)/shard_map/while/body/eval_jaxpr/tbc,tkb->tkc/dot_general | solution.py:38
  104.9 0.7 bitcast_dynamic-update-slice_fusion.2
  106.0 1.0 dynamic-slice_bitcast_fusion.2
  107.0 4.8 %fusion.85 = bf16[512,2,128]{2,1,0:T(2,128)(2,1)} fusion(s32[512,32]{1,0:T(8,128)S(1)} %multiply_subtract_fusion.4, pred[512,32]{1,0:T(8,128)(4,1)S(1)} %get-tuple-element.212, s32[512,32]{1,0:T(8,128)S(1)} %get-tuple-element.213, bf16[512,32]{1,0:T(8,128)(2,1)S(1)} %dynamic-slice_bitcast_fusion.2), kind=kOutput, calls=%fused_computation.5.clone.1 | convolution fusion | flops 10715136 | bytes 442368 | tf_op jit(solution)/shard_map/while/body/eval_jaxpr/tkb,tkc->tbc/dot_general | solution.py:29
  111.8 1.3 convolution_add_fusion.2
  113.2 1.2 fusion.86
  114.4 13.0 %multiply_reduce_fusion.3 = f32[512,32]{1,0:T(8,128)S(1)} fusion(s32[512,32]{1,0:T(8,128)} %copy-done.3, f32[512,2,128]{2,0,1:T(8,128)S(1)} %fusion.86, pred[512,32]{1,0:T(8,128)(4,1)S(1)} %get-tuple-element.212, s32[512,32]{1,0:T(8,128)} %copy-done.2), kind=kOutput, calls=%fused_computation.clone.1 | convolution fusion | flops 60866560 | bytes 737280 | tf_op jit(solution)/shard_map/while/body/eval_jaxpr/tbc,tkb->tkc/dot_general | solution.py:38
  127.4 0.7 bitcast_dynamic-update-slice_fusion.2
  128.5 1.0 dynamic-slice_bitcast_fusion.2
  129.5 4.8 %fusion.85 = bf16[512,2,128]{2,1,0:T(2,128)(2,1)} fusion(s32[512,32]{1,0:T(8,128)S(1)} %multiply_subtract_fusion.4, pred[512,32]{1,0:T(8,128)(4,1)S(1)} %get-tuple-element.212, s32[512,32]{1,0:T(8,128)S(1)} %get-tuple-element.213, bf16[512,32]{1,0:T(8,128)(2,1)S(1)} %dynamic-slice_bitcast_fusion.2), kind=kOutput, calls=%fused_computation.5.clone.1 | convolution fusion | flops 10715136 | bytes 442368 | tf_op jit(solution)/shard_map/while/body/eval_jaxpr/tkb,tkc->tbc/dot_general | solution.py:29
  134.3 1.3 convolution_add_fusion.2
  135.7 1.2 fusion.86
  136.9 13.0 %multiply_reduce_fusion.3 = f32[512,32]{1,0:T(8,128)S(1)} fusion(s32[512,32]{1,0:T(8,128)} %copy-done.3, f32[512,2,128]{2,0,1:T(8,128)S(1)} %fusion.86, pred[512,32]{1,0:T(8,128)(4,1)S(1)} %get-tuple-element.212, s32[512,32]{1,0:T(8,128)} %copy-done.2), kind=kOutput, calls=%fused_computation.clone.1 | convolution fusion | flops 60866560 | bytes 737280 | tf_op jit(solution)/shard_map/while/body/eval_jaxpr/tbc,tkb->tkc/dot_general | solution.py:38
  149.9 0.7 bitcast_dynamic-update-slice_fusion.2
  150.6 2.3 copy.42
  153.8 77.3 %reduce-scatter.4.cloned.1.call-done = f32[128,32]{0,1:T(8,128)} async-done(((f32[2048,32]{0,1:T(8,128)}), f32[128,32]{0,1:T(8,128)}) %reduce-scatter.4.cloned.1.call-update) | async-done | bytes 16400 | tf_op jit(solution)/shard_map/reduce_scatter | solution.py:76
  231.0 46.3 %psum.7 = f32[128,32]{0,1:T(8,128)S(1)} all-reduce(f32[128,32]{0,1:T(8,128)} %reduce-scatter.4.cloned.1.call-done), channel_id=1, replica_groups=mesh['dp'=16,'mem'=16] {'mem'}, use_global_device_ids=true, to_apply=%region_4.5 | all-reduce | flops 4096 | bytes 32768 | tf_op jit(solution)/shard_map/psum | solution.py:76
  277.5 0.6 copy-done.7
  278.1 1.5 fusion.27
  279.9 2.3 fusion.28
  282.4 0.8 stack_reshape.8
  283.3 0.9 fusion.41
  284.3 1.4 fusion.29
  285.9 1.2 fusion.65
  287.2 0.7 dynamic-slice
  288.5 90.3 %all-reduce.3.cloned.1.call-done = f32[2,64,512]{2,1,0:T(8,128)} async-done(((f32[2,64,512]{2,1,0:T(8,128)}), f32[2,64,512]{2,1,0:T(8,128)}) %all-reduce.3.cloned.1.call-update) | async-done | bytes 262160
  378.8 0.8 constant_dynamic-slice_fusion
  379.6 18.1 %all_gather.15 = f32[2,64,512]{2,0,1:T(2,128)S(1)} all-gather(f32[2,4,512]{2,0,1:T(2,128)S(1)} %copy.51), channel_id=1, replica_groups=mesh['dp'=16,'mem'=16] {'mem'}, dimensions={1}, use_global_device_ids=true | all-gather | bytes 278528 | tf_op jit(solution)/shard_map/all_gather | solution.py:118
  397.7 0.8 copy.53
  398.5 62.8 %reduce-scatter.6.cloned.1.call-done = f32[64,256]{1,0:T(8,128)} async-done(((f32[1024,256]{1,0:T(8,128)}), f32[64,256]{1,0:T(8,128)}) %reduce-scatter.6.cloned.1.call-update) | async-done | bytes 65552 | tf_op jit(solution)/shard_map/reduce_scatter | solution.py:110
  (66 shorter events, 3.6 us)
Async XLA Ops:
  7.2 277.1 %copy-start = (bf16[2,1024,512]{2,1,0:T(8,128)(2,1)S(1)}, bf16[2,1024,512]{2,1,0:T(8,128)(2,1)}, u32[]{:S(2)}) copy-start(bf16[2,1024,512]{2,1,0:T(8,128)(2,1)} %param.16) | copy-start | bytes 6291460
  7.2 53.4 %all-gather.2.cloned.1.call-start = ((), (), s32[]{:S(2)}) async-start(), calls=%async_computation.2 | async-start | bytes 1114112 | tf_op jit(solution)/shard_map/all_gather | solution.py:57
  7.9 223.1 %reduce-scatter.4.cloned.1.call-start = ((), (), s32[]{:S(2)}) async-start(), calls=%async_computation.3 | async-start | bytes 278528 | tf_op jit(solution)/shard_map/reduce_scatter | solution.py:76
  60.5 92.5 %copy-start.6 = (s32[2,128,32]{1,2,0:T(8,128)S(1)}, s32[2,128,32]{1,2,0:T(8,128)}, u32[]{:S(2)}) copy-start(s32[2,128,32]{1,2,0:T(8,128)} %param.14) | copy-start | bytes 98308
  60.8 6.0 %copy-start.2 = (s32[512,32]{1,0:T(8,128)}, s32[512,32]{1,0:T(8,128)S(1)}, u32[]{:S(2)}) copy-start(s32[512,32]{1,0:T(8,128)S(1)} %get-tuple-element.213) | copy-start | bytes 196612 | tf_op jit(solution)/shard_map/while
  61.0 5.8 %copy-start.3 = (s32[512,32]{1,0:T(8,128)}, s32[512,32]{1,0:T(8,128)S(1)}, u32[]{:S(2)}) copy-start(s32[512,32]{1,0:T(8,128)S(1)} %multiply_subtract_fusion.4) | copy-start | bytes 196612 | tf_op jit(solution)/shard_map/while
  83.3 6.0 %copy-start.2 = (s32[512,32]{1,0:T(8,128)}, s32[512,32]{1,0:T(8,128)S(1)}, u32[]{:S(2)}) copy-start(s32[512,32]{1,0:T(8,128)S(1)} %get-tuple-element.213) | copy-start | bytes 196612 | tf_op jit(solution)/shard_map/while
  83.5 5.8 %copy-start.3 = (s32[512,32]{1,0:T(8,128)}, s32[512,32]{1,0:T(8,128)S(1)}, u32[]{:S(2)}) copy-start(s32[512,32]{1,0:T(8,128)S(1)} %multiply_subtract_fusion.4) | copy-start | bytes 196612 | tf_op jit(solution)/shard_map/while
  105.8 6.0 %copy-start.2 = (s32[512,32]{1,0:T(8,128)}, s32[512,32]{1,0:T(8,128)S(1)}, u32[]{:S(2)}) copy-start(s32[512,32]{1,0:T(8,128)S(1)} %get-tuple-element.213) | copy-start | bytes 196612 | tf_op jit(solution)/shard_map/while
  106.0 5.8 %copy-start.3 = (s32[512,32]{1,0:T(8,128)}, s32[512,32]{1,0:T(8,128)S(1)}, u32[]{:S(2)}) copy-start(s32[512,32]{1,0:T(8,128)S(1)} %multiply_subtract_fusion.4) | copy-start | bytes 196612 | tf_op jit(solution)/shard_map/while
  128.3 6.0 %copy-start.2 = (s32[512,32]{1,0:T(8,128)}, s32[512,32]{1,0:T(8,128)S(1)}, u32[]{:S(2)}) copy-start(s32[512,32]{1,0:T(8,128)S(1)} %get-tuple-element.213) | copy-start | bytes 196612 | tf_op jit(solution)/shard_map/while
  128.5 5.8 %copy-start.3 = (s32[512,32]{1,0:T(8,128)}, s32[512,32]{1,0:T(8,128)S(1)}, u32[]{:S(2)}) copy-start(s32[512,32]{1,0:T(8,128)S(1)} %multiply_subtract_fusion.4) | copy-start | bytes 196612 | tf_op jit(solution)/shard_map/while
  150.6 129.2 %copy-start.1 = (f32[256,256]{1,0:T(8,128)}, f32[256,256]{1,0:T(8,128)S(1)}, u32[]{:S(2)}) copy-start(f32[256,256]{1,0:T(8,128)S(1)} %get-tuple-element.135) | copy-start | bytes 786436
  150.6 126.7 %copy-start.5 = (f32[128,32]{0,1:T(8,128)S(1)}, f32[128,32]{0,1:T(8,128)}, u32[]{:S(2)}) copy-start(f32[128,32]{0,1:T(8,128)} %param.13) | copy-start | bytes 49156
  153.0 225.8 %all-reduce.3.cloned.1.call-start = ((), (), s32[]{:S(2)}) async-start(), calls=%async_computation.5 | async-start | bytes 524288
  277.5 0.6 copy-start.7
  279.6 3.7 copy-start.4
  283.3 2.6 copy-start.8
  284.2 177.0 %reduce-scatter.6.cloned.1.call-start = ((), (), s32[]{:S(2)}) async-start(), calls=%async_computation.4 | async-start | bytes 1114112 | tf_op jit(solution)/shard_map/reduce_scatter | solution.py:110
  285.7 1.5 copy-start.9
Sparse Core Ops, SparseCore 0:
  10.4 50.0 all-gather.1
  153.1 77.8 reduce-scatter.3
  284.3 94.4 all-reduce.2
  382.7 78.4 reduce-scatter.5
where the time goes:
time: 469 us; the launch traced here: 468 us
  waiting for transfers between devices  233 us (50%)
  blocking collectives  112 us (24%)
  matrix products  88.4 us (19%)
  local copies, waits for them, and re-layouts  16.8 us (4%)
  between operations  14.6 us (3%)
    unnamed x5, waiting for transfers between devices  91.1 us
    reduce_scatter x1, waiting for transfers between devices, body(): lax.psum_scatter(slot_all, 'dp', scatter_dimension=0, tiled=True)  77.3 us
    reduce_scatter x1, waiting for transfers between devices, body(): lax.psum_scatter(lax.dot_general(dquery, layer_input, (((0,), (0,)), ((),...  62.8 us
    dot_general x4, matrix products, value_block(): jnp.einsum('tbc,tkb->tkc', scores, block_hot.astype(jnp.float32), precisi...  51.8 us
    psum x1, blocking collectives, body(): lax.psum(lax.psum_scatter(slot_all, 'dp', scatter_dimension=0, tiled=True...  46.3 us
    all_gather x1, blocking collectives, body(): row_ids = lax.all_gather(slot_rows, 'dp', axis=0, tiled=True)  25.9 us
    all_gather x1, blocking collectives, body(): row_weights = lax.all_gather(vweights, 'dp', axis=0, tiled=True)  22 us
    dot_general x4, matrix products, value_block(): jnp.einsum('tkb,tkc->tbc', weighted, within_hot, preferred_element_type=j...  19 us
  transfers between devices with their start and end apart: 4, of which 4 were waited for; matrix products, arithmetic and copies ran while one was open for 2% of the time, Pallas kernels for 0%

commit v1 on v0

--- a/solution.py
+++ b/solution.py
@@ -73,7 +73,12 @@
     value_acc, slot_terms = lax.scan(one_block, value_acc, stacked)
     slot_all = slot_terms.reshape(row_count, slot_count)
     value_grad, slot_all = (value_acc, slot_all)
-    slot_grad = lax.psum(lax.psum_scatter(slot_all, "dp", scatter_dimension=0, tiled=True), "mem")
+    slot_grad = jnp.sum(
+        lax.all_gather(
+            lax.psum_scatter(slot_all, "dp", scatter_dimension=0, tiled=True), axis_name="mem"
+        ),
+        axis=0,
+    )
     centered = slot_grad - jnp.sum(weights * slot_grad, axis=1, keepdims=True)
     score_grad = weights * centered
     own_count = score_grad.shape[0]

time: 469 us -> 439 us (0.936)
  blocking collectives: 112 us -> 86.6 us
  waiting for transfers between devices: 233 us -> 226 us
    psum x1 -> x0, blocking collectives: 46.3 us -> none  [body(): lax.psum(lax.psum_scatter(slot_all, 'dp', scatter_dimension=0, tiled=True...]
    all_gather x0 -> x1, blocking collectives: none -> 20.6 us  [body(): lax.all_gather(lax.psum_scatter(slot_all, 'dp', scatter_dimension=0, tile...]
  transfers between devices with their start and end apart: 4 -> 4, of which waited for: 4 -> 4; matrix products, arithmetic and copies ran while one was open for 2% -> 3% of each run, Pallas kernels for 0% -> 0%
where the time goes in v1:
time: 439 us; the launch traced here: 438 us
  waiting for transfers between devices  226 us (51%)
  matrix products  89.3 us (20%)
  blocking collectives  86.6 us (20%)
  local copies, waits for them, and re-layouts  17.6 us (4%)
  between operations  14.7 us (3%)
    unnamed x5, waiting for transfers between devices  88.4 us
    reduce_scatter x1, waiting for transfers between devices, body(): lax.psum_scatter(slot_all, 'dp', scatter_dimension=0, tiled=True)  72.7 us
    reduce_scatter x1, waiting for transfers between devices, body(): lax.psum_scatter(lax.dot_general(dquery, layer_input, (((0,), (0,)), ((),...  62.8 us
    dot_general x4, matrix products, value_block(): jnp.einsum('tbc,tkb->tkc', scores, block_hot.astype(jnp.float32), precisi...  51.8 us
    all_gather x1, blocking collectives, body(): row_ids = lax.all_gather(slot_rows, 'dp', axis=0, tiled=True)  25.9 us
    all_gather x1, blocking collectives, body(): row_weights = lax.all_gather(vweights, 'dp', axis=0, tiled=True)  22 us
    all_gather x1, blocking collectives, body(): lax.all_gather(lax.psum_scatter(slot_all, 'dp', scatter_dimension=0, tile...  20.6 us
    dot_general x4, matrix products, value_block(): jnp.einsum('tkb,tkc->tbc', weighted, within_hot, preferred_element_type=j...  19 us
  transfers between devices with their start and end apart: 4, of which 4 were waited for; matrix products, arithmetic and copies ran while one was open for 3% of the time, Pallas kernels for 0%

profile of v1, /device:TPU:2, one launch (start us, length us, event | category | flops | bytes accessed | tf_op | source)
XLA Modules:
  0.0 438.3 jit_solution(14544853880277708601)
XLA Ops:
  8.0 25.9 %all_gather.18 = s32[2048,32]{0,1:T(8,128)} all-gather(s32[128,32]{0,1:T(8,128)} %param.12), channel_id=1, replica_groups=mesh['dp'=16,'mem'=16] {'dp'}, dimensions={0}, use_global_device_ids=true | all-gather | bytes 278528 | tf_op jit(solution)/shard_map/all_gather | solution.py:58
  33.8 1.3 copy.53
  35.1 0.7 convert_element_type.41
  35.9 22.0 %all_gather.19 = bf16[2048,32]{0,1:T(8,128)(2,1)S(1)} all-gather(bf16[128,32]{0,1:T(8,128)(2,1)S(1)} %convert_element_type.41), channel_id=1, replica_groups=mesh['dp'=16,'mem'=16] {'dp'}, dimensions={0}, use_global_device_ids=true | all-gather | bytes 139264 | tf_op jit(solution)/shard_map/all_gather | solution.py:59
  57.8 1.0 copy.54
  58.8 1.7 all-gather.3.cloned.1.call-done
  60.5 90.0 %while.15 = (s32[]{:T(128)}, f32[256,256]{1,0:T(8,128)S(1)}, f32[4,512,32]{2,1,0:T(8,128)}, s32[4,512,32]{2,1,0:T(8,128)S(1)}, s32[]{:T(128)}, /*index=5*/bf16[4...) while((s32[]{:T(128)}, f32[256,256]{1,0:T(8,128)S(1)}, ...), condition=%wide.region_2.3_spmd.clone, body=%wide.region_0.2_spmd.clone.sunk | while | flops 206569472 | bytes 4358351 | solution.py:73
  61.0 1.0 dynamic-slice_bitcast_fusion.2
  62.0 4.8 %fusion.85 = bf16[512,2,128]{2,1,0:T(2,128)(2,1)} fusion(s32[512,32]{1,0:T(8,128)S(1)} %multiply_subtract_fusion.4, pred[512,32]{1,0:T(8,128)(4,1)S(1)} %get-tuple-element.215, s32[512,32]{1,0:T(8,128)S(1)} %get-tuple-element.216, bf16[512,32]{1,0:T(8,128)(2,1)S(1)} %dynamic-slice_bitcast_fusion.2), kind=kOutput, calls=%fused_computation.5.clone.1 | convolution fusion | flops 10715136 | bytes 442368 | tf_op jit(solution)/shard_map/while/body/eval_jaxpr/tkb,tkc->tbc/dot_general | solution.py:29
  66.8 1.3 convolution_add_fusion.2
  68.1 1.2 fusion.86
  69.4 13.0 %multiply_reduce_fusion.3 = f32[512,32]{1,0:T(8,128)S(1)} fusion(s32[512,32]{1,0:T(8,128)} %copy-done.3, f32[512,2,128]{2,0,1:T(8,128)S(1)} %fusion.86, pred[512,32]{1,0:T(8,128)(4,1)S(1)} %get-tuple-element.215, s32[512,32]{1,0:T(8,128)} %copy-done.2), kind=kOutput, calls=%fused_computation.clone.1 | convolution fusion | flops 60866560 | bytes 737280 | tf_op jit(solution)/shard_map/while/body/eval_jaxpr/tbc,tkb->tkc/dot_general | solution.py:38
  82.3 0.7 bitcast_dynamic-update-slice_fusion.2
  83.5 1.0 dynamic-slice_bitcast_fusion.2
  84.5 4.8 %fusion.85 = bf16[512,2,128]{2,1,0:T(2,128)(2,1)} fusion(s32[512,32]{1,0:T(8,128)S(1)} %multiply_subtract_fusion.4, pred[512,32]{1,0:T(8,128)(4,1)S(1)} %get-tuple-element.215, s32[512,32]{1,0:T(8,128)S(1)} %get-tuple-element.216, bf16[512,32]{1,0:T(8,128)(2,1)S(1)} %dynamic-slice_bitcast_fusion.2), kind=kOutput, calls=%fused_computation.5.clone.1 | convolution fusion | flops 10715136 | bytes 442368 | tf_op jit(solution)/shard_map/while/body/eval_jaxpr/tkb,tkc->tbc/dot_general | solution.py:29
  89.3 1.3 convolution_add_fusion.2
  90.6 1.2 fusion.86
  91.9 13.0 %multiply_reduce_fusion.3 = f32[512,32]{1,0:T(8,128)S(1)} fusion(s32[512,32]{1,0:T(8,128)} %copy-done.3, f32[512,2,128]{2,0,1:T(8,128)S(1)} %fusion.86, pred[512,32]{1,0:T(8,128)(4,1)S(1)} %get-tuple-element.215, s32[512,32]{1,0:T(8,128)} %copy-done.2), kind=kOutput, calls=%fused_computation.clone.1 | convolution fusion | flops 60866560 | bytes 737280 | tf_op jit(solution)/shard_map/while/body/eval_jaxpr/tbc,tkb->tkc/dot_general | solution.py:38
  106.0 1.0 dynamic-slice_bitcast_fusion.2
  107.0 4.8 %fusion.85 = bf16[512,2,128]{2,1,0:T(2,128)(2,1)} fusion(s32[512,32]{1,0:T(8,128)S(1)} %multiply_subtract_fusion.4, pred[512,32]{1,0:T(8,128)(4,1)S(1)} %get-tuple-element.215, s32[512,32]{1,0:T(8,128)S(1)} %get-tuple-element.216, bf16[512,32]{1,0:T(8,128)(2,1)S(1)} %dynamic-slice_bitcast_fusion.2), kind=kOutput, calls=%fused_computation.5.clone.1 | convolution fusion | flops 10715136 | bytes 442368 | tf_op jit(solution)/shard_map/while/body/eval_jaxpr/tkb,tkc->tbc/dot_general | solution.py:29
  111.8 1.3 convolution_add_fusion.2
  113.1 1.2 fusion.86
  114.4 13.0 %multiply_reduce_fusion.3 = f32[512,32]{1,0:T(8,128)S(1)} fusion(s32[512,32]{1,0:T(8,128)} %copy-done.3, f32[512,2,128]{2,0,1:T(8,128)S(1)} %fusion.86, pred[512,32]{1,0:T(8,128)(4,1)S(1)} %get-tuple-element.215, s32[512,32]{1,0:T(8,128)} %copy-done.2), kind=kOutput, calls=%fused_computation.clone.1 | convolution fusion | flops 60866560 | bytes 737280 | tf_op jit(solution)/shard_map/while/body/eval_jaxpr/tbc,tkb->tkc/dot_general | solution.py:38
  127.3 0.7 bitcast_dynamic-update-slice_fusion.2
  128.5 1.0 dynamic-slice_bitcast_fusion.2
  129.5 4.8 %fusion.85 = bf16[512,2,128]{2,1,0:T(2,128)(2,1)} fusion(s32[512,32]{1,0:T(8,128)S(1)} %multiply_subtract_fusion.4, pred[512,32]{1,0:T(8,128)(4,1)S(1)} %get-tuple-element.215, s32[512,32]{1,0:T(8,128)S(1)} %get-tuple-element.216, bf16[512,32]{1,0:T(8,128)(2,1)S(1)} %dynamic-slice_bitcast_fusion.2), kind=kOutput, calls=%fused_computation.5.clone.1 | convolution fusion | flops 10715136 | bytes 442368 | tf_op jit(solution)/shard_map/while/body/eval_jaxpr/tkb,tkc->tbc/dot_general | solution.py:29
  134.3 1.3 convolution_add_fusion.2
  135.6 1.2 fusion.86
  136.9 13.0 %multiply_reduce_fusion.3 = f32[512,32]{1,0:T(8,128)S(1)} fusion(s32[512,32]{1,0:T(8,128)} %copy-done.3, f32[512,2,128]{2,0,1:T(8,128)S(1)} %fusion.86, pred[512,32]{1,0:T(8,128)(4,1)S(1)} %get-tuple-element.215, s32[512,32]{1,0:T(8,128)} %copy-done.2), kind=kOutput, calls=%fused_computation.clone.1 | convolution fusion | flops 60866560 | bytes 737280 | tf_op jit(solution)/shard_map/while/body/eval_jaxpr/tbc,tkb->tkc/dot_general | solution.py:38
  149.8 0.7 bitcast_dynamic-update-slice_fusion.2
  151.5 0.8 add_select_fusion.2
  153.0 0.7 multiply_subtract_fusion.2
  153.7 0.7 copy.60
  155.2 0.7 copy.64
  155.9 0.7 copy.62
  156.6 72.7 %reduce-scatter.4.cloned.1.call-done = f32[128,32]{1,0:T(8,128)} async-done(((f32[2048,32]{1,0:T(8,128)}), f32[128,32]{1,0:T(8,128)}) %reduce-scatter.4.cloned.1.call-update) | async-done | bytes 16400 | tf_op jit(solution)/shard_map/reduce_scatter | solution.py:78
  229.3 20.6 %all-gather = f32[2048,32]{1,0:T(8,128)S(1)} all-gather(f32[128,32]{1,0:T(8,128)} %reduce-scatter.4.cloned.1.call-done), channel_id=2, replica_groups=mesh['dp'=16,'mem'=16] {'mem'}, dimensions={0}, use_global_device_ids=true | all-gather | bytes 278528 | tf_op jit(solution)/shard_map/all_gather | solution.py:77
  250.3 2.3 fusion.27
  253.1 2.3 fusion.28
  255.6 0.8 stack_reshape.8
  256.4 0.9 fusion.41
  257.4 1.4 fusion.29
  259.0 1.3 fusion.65
  261.6 87.7 %all-reduce.3.cloned.1.call-done = f32[2,64,512]{2,1,0:T(8,128)} async-done(((f32[2,64,512]{2,1,0:T(8,128)}), f32[2,64,512]{2,1,0:T(8,128)}) %all-reduce.3.cloned.1.call-update) | async-done | bytes 262160
  349.3 0.8 constant_dynamic-slice_fusion
  350.1 18.1 %all_gather.23 = f32[2,64,512]{2,0,1:T(2,128)S(1)} all-gather(f32[2,4,512]{2,0,1:T(2,128)S(1)} %copy.67), channel_id=1, replica_groups=mesh['dp'=16,'mem'=16] {'mem'}, dimensions={1}, use_global_device_ids=true | all-gather | bytes 278528 | tf_op jit(solution)/shard_map/all_gather | solution.py:123
  368.2 0.8 copy.69
  369.0 62.8 %reduce-scatter.6.cloned.1.call-done = f32[64,256]{1,0:T(8,128)} async-done(((f32[1024,256]{1,0:T(8,128)}), f32[64,256]{1,0:T(8,128)}) %reduce-scatter.6.cloned.1.call-update) | async-done | bytes 65552 | tf_op jit(solution)/shard_map/reduce_scatter | solution.py:115
  (74 shorter events, 7.4 us)
Async XLA Ops:
  7.2 250.2 %copy-start = (bf16[2,1024,512]{2,1,0:T(8,128)(2,1)S(1)}, bf16[2,1024,512]{2,1,0:T(8,128)(2,1)}, u32[]{:S(2)}) copy-start(bf16[2,1024,512]{2,1,0:T(8,128)(2,1)} %param.16) | copy-start | bytes 6291460
  7.2 53.4 %all-gather.3.cloned.1.call-start = ((), (), s32[]{:S(2)}) async-start(), calls=%async_computation.2 | async-start | bytes 1114112 | tf_op jit(solution)/shard_map/all_gather | solution.py:57
  7.9 221.4 %reduce-scatter.4.cloned.1.call-start = ((), (), s32[]{:S(2)}) async-start(), calls=%async_computation.3 | async-start | bytes 1114112 | tf_op jit(solution)/shard_map/reduce_scatter | solution.py:78
  60.5 90.1 %copy-start.6 = (s32[2,128,32]{1,2,0:T(8,128)S(1)}, s32[2,128,32]{1,2,0:T(8,128)}, u32[]{:S(2)}) copy-start(s32[2,128,32]{1,2,0:T(8,128)} %param.14) | copy-start | bytes 98308
  60.5 90.2 %copy-start.5 = (f32[128,32]{0,1:T(8,128)S(1)}, f32[128,32]{0,1:T(8,128)}, u32[]{:S(2)}) copy-start(f32[128,32]{0,1:T(8,128)} %param.13) | copy-start | bytes 49156
  60.8 6.0 %copy-start.2 = (s32[512,32]{1,0:T(8,128)}, s32[512,32]{1,0:T(8,128)S(1)}, u32[]{:S(2)}) copy-start(s32[512,32]{1,0:T(8,128)S(1)} %get-tuple-element.216) | copy-start | bytes 196612 | tf_op jit(solution)/shard_map/while
  61.0 5.8 %copy-start.3 = (s32[512,32]{1,0:T(8,128)}, s32[512,32]{1,0:T(8,128)S(1)}, u32[]{:S(2)}) copy-start(s32[512,32]{1,0:T(8,128)S(1)} %multiply_subtract_fusion.4) | copy-start | bytes 196612 | tf_op jit(solution)/shard_map/while
  83.3 6.0 %copy-start.2 = (s32[512,32]{1,0:T(8,128)}, s32[512,32]{1,0:T(8,128)S(1)}, u32[]{:S(2)}) copy-start(s32[512,32]{1,0:T(8,128)S(1)} %get-tuple-element.216) | copy-start | bytes 196612 | tf_op jit(solution)/shard_map/while
  83.5 5.8 %copy-start.3 = (s32[512,32]{1,0:T(8,128)}, s32[512,32]{1,0:T(8,128)S(1)}, u32[]{:S(2)}) copy-start(s32[512,32]{1,0:T(8,128)S(1)} %multiply_subtract_fusion.4) | copy-start | bytes 196612 | tf_op jit(solution)/shard_map/while
  105.8 6.0 %copy-start.2 = (s32[512,32]{1,0:T(8,128)}, s32[512,32]{1,0:T(8,128)S(1)}, u32[]{:S(2)}) copy-start(s32[512,32]{1,0:T(8,128)S(1)} %get-tuple-element.216) | copy-start | bytes 196612 | tf_op jit(solution)/shard_map/while
  106.0 5.8 %copy-start.3 = (s32[512,32]{1,0:T(8,128)}, s32[512,32]{1,0:T(8,128)S(1)}, u32[]{:S(2)}) copy-start(s32[512,32]{1,0:T(8,128)S(1)} %multiply_subtract_fusion.4) | copy-start | bytes 196612 | tf_op jit(solution)/shard_map/while
  128.3 6.0 %copy-start.2 = (s32[512,32]{1,0:T(8,128)}, s32[512,32]{1,0:T(8,128)S(1)}, u32[]{:S(2)}) copy-start(s32[512,32]{1,0:T(8,128)S(1)} %get-tuple-element.216) | copy-start | bytes 196612 | tf_op jit(solution)/shard_map/while
  128.5 5.8 %copy-start.3 = (s32[512,32]{1,0:T(8,128)}, s32[512,32]{1,0:T(8,128)S(1)}, u32[]{:S(2)}) copy-start(s32[512,32]{1,0:T(8,128)S(1)} %multiply_subtract_fusion.4) | copy-start | bytes 196612 | tf_op jit(solution)/shard_map/while
  150.6 99.7 %copy-start.1 = (f32[256,256]{1,0:T(8,128)}, f32[256,256]{1,0:T(8,128)S(1)}, u32[]{:S(2)}) copy-start(f32[256,256]{1,0:T(8,128)S(1)} %get-tuple-element.138) | copy-start | bytes 786436
  150.6 198.7 %all-reduce.3.cloned.1.call-start = ((), (), s32[]{:S(2)}) async-start(), calls=%async_computation.5 | async-start | bytes 524288
  250.2 2.9 copy-start.7
  250.2 2.9 copy-start.8
  250.2 2.9 copy-start.11
  250.3 2.6 copy-start.9
  252.7 3.8 copy-start.4
  256.4 2.6 copy-start.10
  257.4 174.4 %reduce-scatter.6.cloned.1.call-start = ((), (), s32[]{:S(2)}) async-start(), calls=%async_computation.4 | async-start | bytes 1114112 | tf_op jit(solution)/shard_map/reduce_scatter | solution.py:115
  258.8 1.5 copy-start.12
Sparse Core Ops, SparseCore 0:
  10.4 50.0 all-gather.2
  150.7 78.5 reduce-scatter.3
  257.5 91.7 all-reduce.2
  353.2 78.4 reduce-scatter.5
